TPU v7x, 256 devices: a whole 4x4x8 slice. The times are simulated.
256 devices in a mesh: row: 32 (over z_lo, y, core), col: 8 (over z_hi, x).
Axes of the slice: x: 4, y: 4, z: 8 (z_hi: 2, z_lo: 4; z = z_hi * 4 + z_lo), core: 2. Of those that a mesh axis runs over, the one named last changes fastest.
Arguments:
- slab: bfloat16 [32768, 16384], P('row', 'col'), may hold values from -6 to 6
- panel_left: bfloat16 [32768, 512], P('row', 'col'), may hold values from -3 to 3
- panel_top: bfloat16 [512, 16384], P('row', 'col'), may hold values from -3 to 3
- row_bases: bfloat16 [32768, 256], P('row'), may hold values from -0.25 to 0.25
- col_bases: bfloat16 [16384, 256], P('col'), may hold values from -0.25 to 0.25
- row_ranks: int32 [64], P('row'), may hold values from 32 to 256, as said below
- col_ranks: int32 [32], P('col'), may hold values from 32 to 256, as said below
- pivot_inverse: bfloat16 [512, 512], replicated, may hold values from -0.0625 to 0.0625
- pivot_rhs: bfloat16 [512, 4096], P('row', 'col'), may hold values from -6 to 6
- rhs: bfloat16 [32768, 4096], P('row', 'col'), may hold values from -6 to 6
Outputs:
- slab_new: bfloat16 [32768, 16384], P('row', 'col')
- rhs_new: bfloat16 [32768, 4096], P('row', 'col')
Inputs may be any that keep to these rules, and one draw needn't show every extreme that they name: `row_ranks`: each entry is the rank of one tile; the value 256 occurs in every draw. `col_ranks`: each entry is the rank of one tile; the value 256 occurs in every draw.
All inputs are finite; a program needn't handle non-finite values.
Results may differ from a plain program's by a relative error of at most 0.0062.
Values may be sent and summed in bfloat16 or wider, within the bound.
No kernel may reach another device: no remote copies, remote signals or barrier semaphores. Data moves between devices by JAX's collectives and lax.ppermute only.
A program may use at most 128 MiB of HBM per device.

v0:
```python
import jax
import jax.numpy as jnp
from jax import lax
from jax.sharding import PartitionSpec as P


def from_everyone(array, axis):
    copies = jnp.broadcast_to(array, (lax.axis_size(axis), *array.shape))
    return lax.all_to_all(copies, axis, split_axis=0, concat_axis=0, tiled=True)


def joined_along(blocks, dim):
    blocks = jnp.moveaxis(blocks, 0, dim)
    lengths = blocks.shape
    return blocks.reshape(*lengths[:dim], lengths[dim] * lengths[dim + 1], *lengths[dim + 2 :])


def gather_directly(array, axis, dim):
    blocks = from_everyone(array, axis)
    return joined_along(blocks, dim)


def per_device(
    slab,
    panel_left,
    panel_top,
    row_bases,
    col_bases,
    row_ranks,
    col_ranks,
    pivot_inverse,
    pivot_rhs,
    rhs,
):
    tile_order = pivot_inverse.shape[0]
    rank_width = row_bases.shape[1]
    row_count = row_ranks.shape[0]
    column_count = col_ranks.shape[0]
    gain_width = rhs.shape[1]
    levels = jnp.arange(rank_width, dtype=jnp.int32)
    keep_row = (levels[None, :] < row_ranks[:, None]).astype(jnp.float32)
    keep_column = (levels[None, :] < col_ranks[:, None]).astype(jnp.float32)
    left_bases = row_bases.reshape(row_count, tile_order, rank_width)
    right_bases = col_bases.reshape(column_count, tile_order, rank_width)
    left_tiles = panel_left.reshape(row_count, tile_order, panel_left.shape[1])
    part_core = jnp.einsum(
        "tbr,tbc->trc", left_bases, left_tiles, preferred_element_type=jnp.float32
    )
    part_core = (part_core * keep_row[:, :, None]).astype(jnp.bfloat16)
    row_core = gather_directly(part_core, "col", 2)
    shaped = panel_top.reshape(panel_top.shape[0], column_count, tile_order)
    projected = jnp.einsum("pjc,jcr->pjr", shaped, right_bases, preferred_element_type=jnp.float32)
    outgoing = (projected * keep_column[None]).astype(jnp.bfloat16)
    arrived, rhs_rows = (
        lax.all_gather(outgoing, "row", axis=0, tiled=True),
        lax.all_gather(pivot_rhs, "row", axis=0, tiled=True),
    )
    solved = jnp.dot(pivot_inverse, rhs_rows, preferred_element_type=jnp.float32)
    core_block = jnp.einsum(
        "irp,pjs->ijrs", row_core, arrived, preferred_element_type=jnp.float32
    ).astype(jnp.bfloat16)
    spread = jnp.einsum(
        "ibr,ijrs->ijbs", left_bases, core_block, preferred_element_type=jnp.float32
    ).astype(jnp.bfloat16)
    change = jnp.einsum("ijbs,jcs->ibjc", spread, right_bases, preferred_element_type=jnp.float32)
    change = change.reshape(row_count * tile_order, column_count * tile_order)
    slab_new = (slab.astype(jnp.float32) - change).astype(jnp.bfloat16)
    pivot_solution = solved.astype(jnp.bfloat16)
    reduced = jnp.einsum(
        "irp,pg->irg", row_core, pivot_solution, preferred_element_type=jnp.float32
    ).astype(jnp.bfloat16)
    lowered = jnp.einsum("ibr,irg->ibg", left_bases, reduced, preferred_element_type=jnp.float32)
    lowered = lowered.reshape(row_count * tile_order, gain_width)
    rhs_new = (rhs.astype(jnp.float32) - lowered).astype(jnp.bfloat16)
    return (slab_new, rhs_new)


def solution(mesh):
    in_specs = (
        P("row", "col"),
        P("row", "col"),
        P("row", "col"),
        P("row", None),
        P("col", None),
        P("row"),
        P("col"),
        P(),
        P("row", "col"),
        P("row", "col"),
    )
    out_specs = (P("row", "col"), P("row", "col"))
    return jax.shard_map(
        per_device, mesh=mesh, in_specs=in_specs, out_specs=out_specs, check_vma=False
    )
```

profile of v0, /device:TPU:1, one launch (start us, length us, event | category | flops | bytes accessed | tf_op | source)
XLA Modules:
  0.0 118.2 jit_solution(15169704312447534713)
XLA Ops:
  7.2 0.0 copy-start
  7.2 0.0 copy-start.2
  7.2 0.0 all-gather.2.cloned.1.call-start
  7.2 0.8 fusion.16
  8.1 0.3 copy-done
  8.4 1.1 fusion.10
  9.5 0.6 copy.17
  10.1 0.0 all-gather.2.cloned.1.call-update
  10.1 0.7 compare_convert_fusion
  10.9 1.3 %fusion.8 = bf16[2,256,64]{1,2,0:T(8,128)(2,1)S(1)} fusion(bf16[2,512,256]{2,1,0:T(8,128)(2,1)} %bitcast.57, bf16[8,2,8,512]{3,2,1,0:T(8,128)(2,1)} %bitcast.62, f32[2,256]{1,0:T(2,128)S(1)} %compare_convert_fusion), kind=kOutput, calls=%fused_computation.14 | convolution fusion | flops 33619968 | bytes 722944 | tf_op jit(solution)/shard_map/tbr,tbc->trc/dot_general | solution.py:46
  12.2 0.8 broadcast_in_dim.2
  13.0 11.5 %all-to-all-start = ((bf16[8,2,256,64]{2,3,1,0:T(8,128)(2,1)}), bf16[8,2,256,64]{2,3,1,0:T(8,128)(2,1)S(1)}, u32[]{:S(2)}, u32[]{:S(2)}) async-start(bf16[8,2,256,64]{2,3,1,0:T(8,128)(2,1)} %broadcast_in_dim.2), calls=%async_computation | async-start | bytes 1048576 | tf_op jit(solution)/shard_map/all_to_all | solution.py:9
  24.5 46.1 %all_gather.7 = bf16[512,512]{1,0:T(8,128)(2,1)S(1)} all-gather(bf16[16,512]{1,0:T(8,128)(2,1)} %param.18), channel_id=1, replica_groups=mesh['row'=32,'col'=8] {'row'}, dimensions={0}, use_global_device_ids=true | all-gather | bytes 540672 | tf_op jit(solution)/shard_map/all_gather | solution.py:56
  70.6 0.0 copy-done.2
  70.6 1.3 %fusion.6 = bf16[512,512,1]{1,0,2:T(8,128)(2,1)} fusion(bf16[512,512]{1,0:T(8,128)(2,1)S(1)} %copy-done.2, bf16[512,512]{1,0:T(8,128)(2,1)S(1)} %all_gather.7), kind=kOutput, calls=%fused_computation.11 | convolution fusion | flops 268697600 | bytes 1572864 | tf_op jit(solution)/shard_map/dot_general | solution.py:58
  71.9 0.0 all-to-all-done
  71.9 0.8 copy.19
  72.7 2.2 %fusion.7 = f32[2,512,512]{1,2,0:T(8,128)S(1)} fusion(bf16[2,512,256]{2,1,0:T(8,128)(2,1)} %bitcast.58, bf16[2,256,512]{1,2,0:T(8,128)(2,1)} %bitcast.60, bf16[512,512,1]{1,0,2:T(8,128)(2,1)} %fusion.6), kind=kOutput, calls=%fused_computation.12 | convolution fusion | flops 537133056 | bytes 3670016 | tf_op jit(solution)/shard_map/ibr,irg->ibg/dot_general | solution.py:72
  74.9 2.7 %fusion = bf16[1024,512]{1,0:T(8,128)(2,1)} fusion(f32[2,512,512]{1,2,0:T(8,128)S(1)} %fusion.7, bf16[1024,512]{1,0:T(8,128)(2,1)} %param.19), kind=kLoop, calls=%fused_computation.3 | loop fusion | flops 1572864 | bytes 4194304 | tf_op jit(solution)/shard_map/convert_element_type | solution.py:74
  77.6 2.1 %all-gather.2.cloned.1.call-done = bf16[512,4,256]{2,1,0:T(4,128)(2,1)} async-done(((bf16[16,4,256]{2,1,0:T(4,128)(2,1)}), bf16[512,4,256]{2,1,0:T(4,128)(2,1)}) %all-gather.2.cloned.1.call-update) | async-done | bytes 1048592 | tf_op jit(solution)/shard_map/all_gather | solution.py:55
  79.8 2.1 %fusion.5 = bf16[2,4,256,256]{2,3,0,1:T(8,128)(2,1)S(1)} fusion(bf16[2,256,512,1]{1,2,0,3:T(8,128)(2,1)} %bitcast.61, bf16[512,4,256,1]{2,1,0,3:T(4,128)(2,1)} %bitcast.64), kind=kOutput, calls=%fused_computation.8 | convolution fusion | flops 537395200 | bytes 2621440 | tf_op jit(solution)/shard_map/irp,pjs->ijrs/dot_general | solution.py:59
  81.9 6.1 %convolution_bitcast_fusion = f32[2,512,4,512]{3,1,0,2:T(8,128)} fusion(bf16[4,512,256,1]{2,1,3,0:T(8,128)(2,1)S(1)} %bitcast.53, bf16[2,4,256,256]{2,3,0,1:T(8,128)(2,1)S(1)} %fusion.5, bf16[2,512,256,1]{2,1,0,3:T(8,128)(2,1)} %bitcast.59), kind=kOutput, calls=%fused_computation.1 | convolution fusion | flops 1611661312 | bytes 11010048 | tf_op jit(solution)/shard_map/ijbs,jcs->ibjc/dot_general | solution.py:65
  88.0 12.0 %copy.23 = f32[2,512,4,512]{3,2,1,0:T(4,128)} copy(f32[2,512,4,512]{3,1,0,2:T(8,128)} %convolution_bitcast_fusion) | data formatting | bytes 16777216 | tf_op jit(solution)/shard_map/ijbs,jcs->ibjc/transpose | solution.py:65
  100.0 0.0 copy-start.1
  100.0 7.8 %copy.35 = f32[128,8,4,512]{3,1,2,0:T(8,128)S(1)} copy(f32[128,8,4,512]{3,2,1,0:T(4,128)} %bitcast.55) | data formatting | bytes 16777216
  107.8 0.0 copy-done.1
  107.8 3.5 %subtract_convert_fusion = bf16[1024,2048]{1,0:T(8,128)(2,1)} fusion(f32[1024,2048]{1,0:T(8,128)S(1)} %bitcast.56, bf16[1024,2048]{1,0:T(8,128)(2,1)S(1)} %copy-done.1), kind=kLoop, calls=%fused_computation | loop fusion | flops 6291456 | bytes 16777216 | tf_op jit(solution)/shard_map/convert_element_type | solution.py:67
Async XLA Ops:
  7.2 1.2 %copy-start = (bf16[2048,256]{1,0:T(8,128)(2,1)S(1)}, bf16[2048,256]{1,0:T(8,128)(2,1)}, u32[]{:S(2)}) copy-start(bf16[2048,256]{1,0:T(8,128)(2,1)} %param.14) | copy-start | bytes 3145732
  7.2 63.5 %copy-start.2 = (bf16[512,512]{1,0:T(8,128)(2,1)S(1)}, bf16[512,512]{1,0:T(8,128)(2,1)}, u32[]{:S(2)}) copy-start(bf16[512,512]{1,0:T(8,128)(2,1)} %param.17) | copy-start | bytes 1572868
  7.2 72.6 %all-gather.2.cloned.1.call-start = ((), (), s32[]{:S(2)}) async-start(), calls=%async_computation.1 | async-start | bytes 1081344 | tf_op jit(solution)/shard_map/all_gather | solution.py:55
  13.0 58.9 %all-to-all-start = ((bf16[8,2,256,64]{2,3,1,0:T(8,128)(2,1)}), bf16[8,2,256,64]{2,3,1,0:T(8,128)(2,1)S(1)}, u32[]{:S(2)}, u32[]{:S(2)}) async-start(bf16[8,2,256,64]{2,3,1,0:T(8,128)(2,1)} %broadcast_in_dim.2), calls=%async_computation | async-start | bytes 1048576 | tf_op jit(solution)/shard_map/all_to_all | solution.py:9
  100.0 7.9 %copy-start.1 = (bf16[1024,2048]{1,0:T(8,128)(2,1)S(1)}, bf16[1024,2048]{1,0:T(8,128)(2,1)}, u32[]{:S(2)}) copy-start(bf16[1024,2048]{1,0:T(8,128)(2,1)} %param.10) | copy-start | bytes 12582916
Sparse Core Ops, SparseCore 0:
  10.3 69.4 all-gather.1
where the time goes:
time: 119 us; the launch traced here: 118 us
  blocking collectives  46.1 us (39%)
  local copies, waits for them, and re-layouts  22.5 us (19%)
  matrix products  14.1 us (12%)
  between operations  14.1 us (12%)
  starting transfers between devices  11.5 us (10%)
  other arithmetic  7.77 us (7%)
  waiting for transfers between devices  2.16 us (2%)
    all_gather x1, blocking collectives, per_device(): lax.all_gather(pivot_rhs, 'row', axis=0, tiled=True)  46.1 us
    transpose x1, local copies, waits for them, and re-layouts, per_device(): jnp.einsum('ijbs,jcs->ibjc', spread, right_bases, preferred_element_type=...  12 us
    all_to_all x1, starting transfers between devices, from_everyone(): return lax.all_to_all(copies, axis, split_axis=0, concat_axis=0, tiled=True)  11.5 us
    unnamed x7, local copies, waits for them, and re-layouts  8.2 us
    dot_general x1, matrix products, per_device(): jnp.einsum('ijbs,jcs->ibjc', spread, right_bases, preferred_element_type=...  6.11 us
    convert_element_type x1, other arithmetic, per_device(): slab_new = (slab.astype(jnp.float32) - change).astype(jnp.bfloat16)  3.5 us
    convert_element_type x1, other arithmetic, per_device(): rhs_new = (rhs.astype(jnp.float32) - lowered).astype(jnp.bfloat16)  2.7 us
  transfers between devices with their start and end apart: 2, of which 1 were waited for; matrix products, arithmetic and copies ran while one was open for 8% of the time, Pallas kernels for 0%

commit v1 on v0

--- a/solution.py
+++ b/solution.py
@@ -53,7 +53,9 @@
     outgoing = (projected * keep_column[None]).astype(jnp.bfloat16)
     arrived, rhs_rows = (
         lax.all_gather(outgoing, "row", axis=0, tiled=True),
-        lax.all_gather(pivot_rhs, "row", axis=0, tiled=True),
+        jnp.concatenate(
+            lax.all_to_all(jnp.stack([pivot_rhs] * lax.axis_size("row")), "row", 0, 0), axis=0
+        ),
     )
     solved = jnp.dot(pivot_inverse, rhs_rows, preferred_element_type=jnp.float32)
     core_block = jnp.einsum(

time: 119 us -> 126 us (1.059)
  blocking collectives: 46.1 us -> 0 us
  waiting for transfers between devices: 2.16 us -> 40.7 us
  starting transfers between devices: 11.5 us -> 25.3 us
    all_gather x1 -> x0, blocking collectives: 46.1 us -> none  [per_device(): lax.all_gather(pivot_rhs, 'row', axis=0, tiled=True)]
    all_to_all x0 -> x1, waiting for transfers between devices: none -> 15.6 us  [per_device(): lax.all_to_all(jnp.stack([pivot_rhs] * lax.axis_size('row')), 'row', 0, 0)]
    all_gather x1, waiting for transfers between devices: 2.14 us -> 16 us  [per_device(): lax.all_gather(outgoing, 'row', axis=0, tiled=True)]
    all_to_all x0 -> x1, starting transfers between devices: none -> 13.8 us  [per_device(): lax.all_to_all(jnp.stack([pivot_rhs] * lax.axis_size('row')), 'row', 0, 0)]
    all_to_all x1, waiting for transfers between devices: 0.01 us -> 9.11 us  [from_everyone(): return lax.all_to_all(copies, axis, split_axis=0, concat_axis=0, tiled=True)]
    another operation x0 -> x1, local copies, waits for them, and re-layouts: none -> 1.57 us  [per_device(): jnp.stack([pivot_rhs] * lax.axis_size('row'))]
  transfers between devices with their start and end apart: 2 -> 3, of which waited for: 1 -> 3; matrix products, arithmetic and copies ran while one was open for 8% -> 9% of each run, Pallas kernels for 0% -> 0%
where the time goes in v1:
time: 126 us
  waiting for transfers between devices  40.7 us (32%)
  starting transfers between devices  25.3 us (20%)
  local copies, waits for them, and re-layouts  23.7 us (19%)
  between operations  14.1 us (11%)
  matrix products  14 us (11%)
  other arithmetic  7.78 us (6%)
    all_gather x1, waiting for transfers between devices, per_device(): lax.all_gather(outgoing, 'row', axis=0, tiled=True)  16 us
    all_to_all x1, waiting for transfers between devices, per_device(): lax.all_to_all(jnp.stack([pivot_rhs] * lax.axis_size('row')), 'row', 0, 0)  15.6 us
    all_to_all x1, starting transfers between devices, per_device(): lax.all_to_all(jnp.stack([pivot_rhs] * lax.axis_size('row')), 'row', 0, 0)  13.8 us
    transpose x1, local copies, waits for them, and re-layouts, per_device(): jnp.einsum('ijbs,jcs->ibjc', spread, right_bases, preferred_element_type=...  12 us
    all_to_all x1, starting transfers between devices, from_everyone(): return lax.all_to_all(copies, axis, split_axis=0, concat_axis=0, tiled=True)  11.5 us
    all_to_all x1, waiting for transfers between devices, from_everyone(): return lax.all_to_all(copies, axis, split_axis=0, concat_axis=0, tiled=True)  9.11 us
    unnamed x7, local copies, waits for them, and re-layouts  7.86 us
    dot_general x1, matrix products, per_device(): jnp.einsum('ijbs,jcs->ibjc', spread, right_bases, preferred_element_type=...  6.1 us
  transfers between devices with their start and end apart: 3, of which 3 were waited for; matrix products, arithmetic and copies ran while one was open for 9% of the time, Pallas kernels for 0%

profile of v1, /device:TPU:1, one launch (start us, length us, event | category | flops | bytes accessed | tf_op | source)
XLA Modules:
  0.0 125.6 jit_solution(9886060214378824902)
XLA Ops:
  7.2 0.0 copy-start
  7.2 0.0 copy-start.2
  7.2 0.8 compare_convert_fusion
  8.0 1.3 %fusion.8 = bf16[2,256,64]{1,2,0:T(8,128)(2,1)S(1)} fusion(bf16[2,512,256]{2,1,0:T(8,128)(2,1)} %bitcast.58, bf16[8,2,8,512]{3,2,1,0:T(8,128)(2,1)} %bitcast.64, f32[2,256]{1,0:T(2,128)S(1)} %compare_convert_fusion), kind=kOutput, calls=%fused_computation.14 | convolution fusion | flops 33619968 | bytes 722944 | tf_op jit(solution)/shard_map/tbr,tbc->trc/dot_general | solution.py:46
  9.4 0.8 broadcast_in_dim.2
  10.2 11.5 %all-to-all-start = ((bf16[8,2,256,64]{2,3,1,0:T(8,128)(2,1)}), bf16[8,2,256,64]{2,3,1,0:T(8,128)(2,1)S(1)}, u32[]{:S(2)}, u32[]{:S(2)}) async-start(bf16[8,2,256,64]{2,3,1,0:T(8,128)(2,1)} %broadcast_in_dim.2), calls=%async_computation | async-start | bytes 1048576 | tf_op jit(solution)/shard_map/all_to_all | solution.py:9
  21.7 0.0 all-gather.2.cloned.1.call-start
  21.7 0.7 fusion.16
  22.4 0.0 copy-done
  22.4 1.1 fusion.10
  23.5 0.6 copy.17
  24.2 0.0 all-gather.2.cloned.1.call-update
  24.2 9.1 %all-to-all-done = bf16[8,2,256,64]{2,3,1,0:T(8,128)(2,1)S(1)} async-done(((bf16[8,2,256,64]{2,3,1,0:T(8,128)(2,1)}), bf16[8,2,256,64]{2,3,1,0:T(8,128)(2,1)S(1)}, u32[]{:S(2)}, u32[]{:S(2)}) %all-to-all-start) | async-done | bytes 524320 | tf_op jit(solution)/shard_map/all_to_all | solution.py:9
  33.3 1.6 %stack.2 = bf16[32,16,512]{2,1,0:T(8,128)(2,1)} broadcast(bf16[16,512]{1,0:T(8,128)(2,1)} %param.18), dimensions={1,2} | broadcast | bytes 540672 | tf_op jit(solution)/shard_map/stack | solution.py:57
  34.9 13.8 %all-to-all-start.1 = ((bf16[32,16,512]{2,1,0:T(8,128)(2,1)}), bf16[32,16,512]{2,1,0:T(8,128)(2,1)S(1)}, u32[]{:S(2)}, u32[]{:S(2)}) async-start(bf16[32,16,512]{2,1,0:T(8,128)(2,1)} %stack.2), calls=%async_computation.1 | async-start | bytes 1048576 | tf_op jit(solution)/shard_map/all_to_all | solution.py:57
  48.6 0.8 copy.19
  49.5 15.6 %all-to-all-done.1 = bf16[32,16,512]{2,1,0:T(8,128)(2,1)S(1)} async-done(((bf16[32,16,512]{2,1,0:T(8,128)(2,1)}), bf16[32,16,512]{2,1,0:T(8,128)(2,1)S(1)}, u32[]{:S(2)}, u32[]{:S(2)}) %all-to-all-start.1) | async-done | bytes 524320 | tf_op jit(solution)/shard_map/all_to_all | solution.py:57
  65.1 0.0 copy-done.2
  65.1 1.2 fusion.6
  66.3 2.2 %fusion.7 = f32[2,512,512]{1,2,0:T(8,128)S(1)} fusion(bf16[2,512,256]{2,1,0:T(8,128)(2,1)} %bitcast.59, bf16[2,256,512]{1,2,0:T(8,128)(2,1)} %bitcast.61, bf16[512,512,1]{1,0,2:T(8,128)(2,1)} %fusion.6), kind=kOutput, calls=%fused_computation.12 | convolution fusion | flops 537133056 | bytes 3670016 | tf_op jit(solution)/shard_map/ibr,irg->ibg/dot_general | solution.py:74
  68.5 2.7 %fusion = bf16[1024,512]{1,0:T(8,128)(2,1)} fusion(f32[2,512,512]{1,2,0:T(8,128)S(1)} %fusion.7, bf16[1024,512]{1,0:T(8,128)(2,1)} %param.19), kind=kLoop, calls=%fused_computation.3 | loop fusion | flops 1572864 | bytes 4194304 | tf_op jit(solution)/shard_map/convert_element_type | solution.py:76
  71.2 16.0 %all-gather.2.cloned.1.call-done = bf16[512,4,256]{2,1,0:T(4,128)(2,1)} async-done(((bf16[16,4,256]{2,1,0:T(4,128)(2,1)}), bf16[512,4,256]{2,1,0:T(4,128)(2,1)}) %all-gather.2.cloned.1.call-update) | async-done | bytes 1048592 | tf_op jit(solution)/shard_map/all_gather | solution.py:55
  87.2 2.1 %fusion.5 = bf16[2,4,256,256]{2,3,0,1:T(8,128)(2,1)S(1)} fusion(bf16[2,256,512,1]{1,2,0,3:T(8,128)(2,1)} %bitcast.62, bf16[512,4,256,1]{2,1,0,3:T(4,128)(2,1)} %bitcast.66), kind=kOutput, calls=%fused_computation.8 | convolution fusion | flops 537395200 | bytes 2621440 | tf_op jit(solution)/shard_map/irp,pjs->ijrs/dot_general | solution.py:61
  89.3 6.1 %convolution_bitcast_fusion = f32[2,512,4,512]{3,1,0,2:T(8,128)} fusion(bf16[4,512,256,1]{2,1,3,0:T(8,128)(2,1)S(1)} %bitcast.54, bf16[2,4,256,256]{2,3,0,1:T(8,128)(2,1)S(1)} %fusion.5, bf16[2,512,256,1]{2,1,0,3:T(8,128)(2,1)} %bitcast.60), kind=kOutput, calls=%fused_computation.1 | convolution fusion | flops 1611661312 | bytes 11010048 | tf_op jit(solution)/shard_map/ijbs,jcs->ibjc/dot_general | solution.py:67
  95.4 12.0 %copy.23 = f32[2,512,4,512]{3,2,1,0:T(4,128)} copy(f32[2,512,4,512]{3,1,0,2:T(8,128)} %convolution_bitcast_fusion) | data formatting | bytes 16777216 | tf_op jit(solution)/shard_map/ijbs,jcs->ibjc/transpose | solution.py:67
  107.4 0.0 copy-start.1
  107.4 7.8 %copy.35 = f32[128,8,4,512]{3,1,2,0:T(8,128)S(1)} copy(f32[128,8,4,512]{3,2,1,0:T(4,128)} %bitcast.56) | data formatting | bytes 16777216
  115.3 0.0 copy-done.1
  115.3 3.5 %subtract_convert_fusion = bf16[1024,2048]{1,0:T(8,128)(2,1)} fusion(f32[1024,2048]{1,0:T(8,128)S(1)} %bitcast.57, bf16[1024,2048]{1,0:T(8,128)(2,1)S(1)} %copy-done.1), kind=kLoop, calls=%fused_computation | loop fusion | flops 6291456 | bytes 16777216 | tf_op jit(solution)/shard_map/convert_element_type | solution.py:69
Async XLA Ops:
  7.2 15.3 %copy-start = (bf16[2048,256]{1,0:T(8,128)(2,1)S(1)}, bf16[2048,256]{1,0:T(8,128)(2,1)}, u32[]{:S(2)}) copy-start(bf16[2048,256]{1,0:T(8,128)(2,1)} %param.14) | copy-start | bytes 3145732
  7.2 57.9 %copy-start.2 = (bf16[512,512]{1,0:T(8,128)(2,1)S(1)}, bf16[512,512]{1,0:T(8,128)(2,1)}, u32[]{:S(2)}) copy-start(bf16[512,512]{1,0:T(8,128)(2,1)} %param.17) | copy-start | bytes 1572868
  10.2 23.1 %all-to-all-start = ((bf16[8,2,256,64]{2,3,1,0:T(8,128)(2,1)}), bf16[8,2,256,64]{2,3,1,0:T(8,128)(2,1)S(1)}, u32[]{:S(2)}, u32[]{:S(2)}) async-start(bf16[8,2,256,64]{2,3,1,0:T(8,128)(2,1)} %broadcast_in_dim.2), calls=%async_computation | async-start | bytes 1048576 | tf_op jit(solution)/shard_map/all_to_all | solution.py:9
  21.7 65.5 %all-gather.2.cloned.1.call-start = ((), (), s32[]{:S(2)}) async-start(), calls=%async_computation.2 | async-start | bytes 1081344 | tf_op jit(solution)/shard_map/all_gather | solution.py:55
  34.9 30.2 %all-to-all-start.1 = ((bf16[32,16,512]{2,1,0:T(8,128)(2,1)}), bf16[32,16,512]{2,1,0:T(8,128)(2,1)S(1)}, u32[]{:S(2)}, u32[]{:S(2)}) async-start(bf16[32,16,512]{2,1,0:T(8,128)(2,1)} %stack.2), calls=%async_computation.1 | async-start | bytes 1048576 | tf_op jit(solution)/shard_map/all_to_all | solution.py:57
  107.4 7.9 %copy-start.1 = (bf16[1024,2048]{1,0:T(8,128)(2,1)S(1)}, bf16[1024,2048]{1,0:T(8,128)(2,1)}, u32[]{:S(2)}) copy-start(bf16[1024,2048]{1,0:T(8,128)(2,1)} %param.10) | copy-start | bytes 12582916
Sparse Core Ops, SparseCore 0:
  24.3 62.8 all-gather.1
